TPU v7x, 128 devices: a whole 4x4x4 slice. The times are simulated.
128 devices in a mesh: inner: 8 (over x_hi, y), outer: 16 (over x_lo, z, core).
Axes of the slice: x: 4 (x_hi: 2, x_lo: 2; x = x_hi * 2 + x_lo), y: 4, z: 4, core: 2. Of those that a mesh axis runs over, the one named last changes fastest.
Arguments:
- queries: bfloat16 [16, 4096, 768], P('outer', 'inner'), may hold values from -8 to 8
- key_rows: bfloat16 [16, 4096, 768], P('outer', 'inner'), may hold values from -8 to 8
- values: bfloat16 [16, 4096, 768], P('outer', 'inner'), may hold values from -6 to 6
- out_weight: bfloat16 [768, 768], replicated, may hold values from -0.21875 to 0.21875
Outputs:
- attention_out: bfloat16 [16, 4096, 768], P('outer', 'inner')
All inputs are finite; a program needn't handle non-finite values.
Results may differ from a plain program's by a relative error of at most 0.0052.
Values may be sent and summed in bfloat16 or wider, within the bound.
A program may use at most 64 MiB of HBM per device.

v0:
```python
import jax
import jax.numpy as jnp
from jax import lax
from jax.sharding import PartitionSpec as P

HEADS = 12
HEAD_DIM = 64
GSTEP = 64


def partner_2(block, axis, distance):
    count = lax.axis_size(axis)
    route = []
    for low in range(count):
        high = low | 1 << distance
        if high != low and high < count:
            route += [(low, high), (high, low)]
    return lax.ppermute(block, axis, route)


def head_terms(query_part, level_set, scale_factor):
    scores = (
        jnp.einsum("td,nd->tn", query_part, level_set[0], preferred_element_type=jnp.float32)
        * scale_factor
    )
    row_peak = jnp.max(scores, axis=1, keepdims=True)
    expo_rows = jnp.exp(scores - row_peak)
    row_total = jnp.sum(expo_rows, axis=1, keepdims=True)
    weights = expo_rows.astype(jnp.bfloat16)
    numerator = jnp.dot(weights, level_set[1], preferred_element_type=jnp.float32)
    return (row_peak, row_total, numerator)


def merge_levels(all_terms):
    overall_peak = jnp.max(jnp.stack([entry[0] for entry in all_terms]), axis=0)
    numer_sum = jnp.zeros_like(all_terms[0][2])
    denom_sum = jnp.zeros_like(all_terms[0][1])
    for entry in all_terms:
        factor = jnp.exp(entry[0] - overall_peak)
        numer_sum = numer_sum + factor * entry[2]
        denom_sum = denom_sum + factor * entry[1]
    return numer_sum / denom_sum


def local(queries, key_rows, values, out_weight):
    query_rows = queries[0]
    kv_pair = jnp.stack([key_rows[0], values[0]])
    inner_bits = lax.axis_size("inner").bit_length() - 1
    level_sets = [kv_pair]
    current = kv_pair
    for level_bit in range(inner_bits):
        kv_half = current[:, ::2]
        partner = partner_2(kv_half, "inner", level_bit)
        current = jnp.concatenate([kv_half, partner], axis=1)
        level_sets.append(current)
    top_half = level_sets[-1][:, ::2]
    outer_partner = partner_2(top_half, "outer", 0)
    level_sets.append(jnp.concatenate([top_half, outer_partner], axis=1))
    own_rows = kv_pair[:, ::GSTEP]
    global_set = lax.all_gather(own_rows, ("inner", "outer"), axis=1, tiled=True)
    level_sets.append(global_set)
    scale_factor = HEAD_DIM ** (-0.5)

    def per_head(head_index):
        col_start = head_index * HEAD_DIM
        head_query = lax.dynamic_slice_in_dim(query_rows, col_start, HEAD_DIM, 1)
        collected = [
            head_terms(
                head_query,
                lax.dynamic_slice_in_dim(level_set, col_start, HEAD_DIM, 2),
                scale_factor,
            )
            for level_set in level_sets
        ]
        return merge_levels(collected)

    merged = lax.map(per_head, jnp.arange(HEADS, dtype=jnp.int32))
    token_count = query_rows.shape[0]
    attended = merged.transpose(1, 0, 2).reshape(token_count, HEADS * HEAD_DIM).astype(jnp.bfloat16)
    result = jnp.dot(attended, out_weight, preferred_element_type=jnp.float32).astype(jnp.bfloat16)
    return result[None]


def solution(mesh):
    placed = (P("outer", "inner", None), P("outer", "inner", None), P("outer", "inner", None), P())
    return jax.shard_map(
        local, mesh=mesh, in_specs=placed, out_specs=P("outer", "inner", None), check_vma=False
    )
```

profile of v0, /device:TPU:1, one launch (start us, length us, event | category | flops | bytes accessed | tf_op | source)
XLA Modules:
  0.0 506.4 jit_solution(17970265938526461845)
XLA Ops:
  10.4 2.2 collective-permute-start
  12.6 16.9 %collective-permute-done = bf16[2,256,768]{2,1,0:T(8,128)(2,1)S(1)} collective-permute-done((bf16[2,256,768]{2,1,0:T(8,128)(2,1)S(1)}, bf16[2,256,768]{2,1,0:T(8,128)(2,1)S(1)}, u32[]{:S(2)}, u32[]{:S(2)}) %collective-permute-start) | collective-permute-done | bytes 786464 | tf_op jit(solution)/shard_map/ppermute | solution.py:18
  31.2 4.1 collective-permute-start.1
  35.3 17.1 %collective-permute-done.1 = bf16[2,256,768]{2,1,0:T(8,128)(2,1)S(1)} collective-permute-done((bf16[2,256,768]{2,1,0:T(8,128)(2,1)S(1)}, bf16[2,256,768]{2,1,0:T(8,128)(2,1)S(1)}, u32[]{:S(2)}, u32[]{:S(2)}) %collective-permute-start.1) | collective-permute-done | bytes 786464 | tf_op jit(solution)/shard_map/ppermute | solution.py:18
  53.7 6.9 %slice.53 = bf16[2,256,768]{2,1,0:T(8,128)(2,1)S(1)} slice(bf16[2,512,768]{2,1,0:T(8,128)(2,1)} %pad_maximum_fusion.1), slice={[0:2:1], [0:512:2], [0:768:1]} | slice | bytes 1572864 | tf_op jit(solution)/shard_map/slice | solution.py:52
  61.8 18.6 %collective-permute-done.2 = bf16[2,256,768]{2,1,0:T(8,128)(2,1)S(1)} collective-permute-done((bf16[2,256,768]{2,1,0:T(8,128)(2,1)S(1)}, bf16[2,256,768]{2,1,0:T(8,128)(2,1)S(1)}, u32[]{:S(2)}, u32[]{:S(2)}) %collective-permute-start.2) | collective-permute-done | bytes 786464 | tf_op jit(solution)/shard_map/ppermute | solution.py:18
  81.6 6.9 %slice.54 = bf16[2,256,768]{2,1,0:T(8,128)(2,1)S(1)} slice(bf16[2,512,768]{2,1,0:T(8,128)(2,1)} %pad_maximum_fusion.2), slice={[0:2:1], [0:512:2], [0:768:1]} | slice | bytes 1572864 | tf_op jit(solution)/shard_map/slice | solution.py:56
  88.6 3.0 collective-permute-start.3
  91.6 2.1 collective-permute-done.3
  93.7 2.5 pad_maximum_fusion.3
  96.1 143.9 %all-gather.2.cloned.1.call-done = bf16[2,1024,768]{2,1,0:T(8,128)(2,1)} async-done(((bf16[2,8,768]{2,1,0:T(8,128)(2,1)}), bf16[2,1024,768]{2,1,0:T(8,128)(2,1)}) %all-gather.2.cloned.1.call-update) | async-done | bytes 3145744 | tf_op jit(solution)/shard_map/all_gather | solution.py:60
  240.0 256.7 %while.10 = (s32[]{:T(128)}, bf16[12,512,64]{1,2,0:T(8,128)(2,1)}, s32[12]{0:T(128)S(1)}, bf16[512,768]{1,0:T(8,128)(2,1)}, bf16[2,512,768]{2,1,0:T(8,128)(2,1)}...) while((s32[]{:T(128)}, bf16[12,512,64]{1,2,0:T(8,128)(2,1)}, ...), condition=%wide.region_13.0_spmd, body=%wide.region_0.13_spmd.sunk | while | flops 482219008 | bytes 72330264 | solution.py:77
  242.7 1.7 fusion.90
  249.6 1.8 multiply_reduce_fusion.2
  253.6 1.6 fusion.95
  257.7 1.7 convolution_multiply_fusion.13
  259.4 2.0 fusion.98
  264.1 1.7 fusion.90
  271.0 1.8 multiply_reduce_fusion.2
  275.0 1.6 fusion.95
  279.1 1.7 convolution_multiply_fusion.13
  280.8 2.0 fusion.98
  285.5 1.7 fusion.90
  292.4 1.8 multiply_reduce_fusion.2
  296.3 1.6 fusion.95
  300.5 1.7 convolution_multiply_fusion.13
  302.2 2.0 fusion.98
  306.9 1.7 fusion.90
  313.8 1.8 multiply_reduce_fusion.2
  321.9 1.7 convolution_multiply_fusion.13
  323.6 2.0 fusion.98
  328.3 1.7 fusion.90
  335.2 1.8 multiply_reduce_fusion.2
  343.3 1.7 convolution_multiply_fusion.13
  345.0 2.0 fusion.98
  349.7 1.7 fusion.90
  356.5 1.8 multiply_reduce_fusion.2
  364.7 1.7 convolution_multiply_fusion.13
  366.4 2.0 fusion.98
  371.0 1.7 fusion.90
  377.9 1.8 multiply_reduce_fusion.2
  386.1 1.7 convolution_multiply_fusion.13
  387.8 2.0 fusion.98
  392.4 1.7 fusion.90
  399.3 1.8 multiply_reduce_fusion.2
  407.5 1.7 convolution_multiply_fusion.13
  409.1 2.0 fusion.98
  413.8 1.7 fusion.90
  420.7 1.8 multiply_reduce_fusion.2
  428.9 1.7 convolution_multiply_fusion.13
  430.5 2.0 fusion.98
  435.2 1.7 fusion.90
  442.1 1.8 multiply_reduce_fusion.2
  450.2 1.7 convolution_multiply_fusion.13
  451.9 2.0 fusion.98
  456.6 1.7 fusion.90
  463.5 1.8 multiply_reduce_fusion.2
  471.6 1.7 convolution_multiply_fusion.13
  473.3 2.0 fusion.98
  478.0 1.7 fusion.90
  484.9 1.8 multiply_reduce_fusion.2
  493.0 1.7 convolution_multiply_fusion.13
  494.7 2.0 fusion.98
  496.7 2.8 fusion.53
  (424 shorter events, 165.2 us)
Async XLA Ops:
  6.5 490.1 %copy-start = (bf16[768,768]{1,0:T(8,128)(2,1)S(1)}, bf16[768,768]{1,0:T(8,128)(2,1)}, u32[]{:S(2)}) copy-start(bf16[768,768]{1,0:T(8,128)(2,1)} %param.9) | copy-start | bytes 3538948
  6.5 233.5 %all-gather.2.cloned.1.call-start = ((), (), s32[]{:S(2)}) async-start(), calls=%async_computation | async-start | bytes 3170304 | tf_op jit(solution)/shard_map/all_gather | solution.py:60
  8.1 4.6 copy-start.11
  10.4 19.1 %collective-permute-start = (bf16[2,256,768]{2,1,0:T(8,128)(2,1)S(1)}, bf16[2,256,768]{2,1,0:T(8,128)(2,1)S(1)}, u32[]{:S(2)}, u32[]{:S(2)}) collective-permute-start(bf16[2,256,768]{2,1,0:T(8,128)(2,1)S(1)} %slice.51), channel_id=1, source_target_pairs={{0,16},{16,0},{32,48},{48,32},{64,80},{80,64},{96,112},{112,96},{1... | collective-permute-start | bytes 2359304 | tf_op jit(solution)/shard_map/ppermute | solution.py:18
  31.2 21.2 %collective-permute-start.1 = (bf16[2,256,768]{2,1,0:T(8,128)(2,1)S(1)}, bf16[2,256,768]{2,1,0:T(8,128)(2,1)S(1)}, u32[]{:S(2)}, u32[]{:S(2)}) collective-permute-start(bf16[2,256,768]{2,1,0:T(8,128)(2,1)S(1)} %slice.52), channel_id=1, source_target_pairs={{0,32},{32,0},{16,48},{48,16},{64,96},{96,64},{80,112},{112,80},{1... | collective-permute-start | bytes 2359304 | tf_op jit(solution)/shard_map/ppermute | solution.py:18
  60.6 19.8 %collective-permute-start.2 = (bf16[2,256,768]{2,1,0:T(8,128)(2,1)S(1)}, bf16[2,256,768]{2,1,0:T(8,128)(2,1)S(1)}, u32[]{:S(2)}, u32[]{:S(2)}) collective-permute-start(bf16[2,256,768]{2,1,0:T(8,128)(2,1)S(1)} %slice.53), channel_id=1, source_target_pairs={{0,64},{64,0},{16,80},{80,16},{32,96},{96,32},{48,112},{112,48},{1... | collective-permute-start | bytes 2359304 | tf_op jit(solution)/shard_map/ppermute | solution.py:18
  88.6 5.1 %collective-permute-start.3 = (bf16[2,256,768]{2,1,0:T(8,128)(2,1)S(1)}, bf16[2,256,768]{2,1,0:T(8,128)(2,1)}, u32[]{:S(2)}, u32[]{:S(2)}) collective-permute-start(bf16[2,256,768]{2,1,0:T(8,128)(2,1)S(1)} %slice.54), channel_id=1, source_target_pairs={{0,1},{1,0},{2,3},{3,2},{4,5},{5,4},{6,7},{7,6},{8,9},{9,8},{10,11... | collective-permute-start | bytes 2359304 | tf_op jit(solution)/shard_map/ppermute | solution.py:18
  240.0 6.1 %copy-start.9 = (bf16[2,512,768]{2,1,0:T(8,128)(2,1)}, bf16[2,512,768]{2,1,0:T(8,128)(2,1)S(1)}, u32[]{:S(2)}) copy-start(bf16[2,512,768]{2,1,0:T(8,128)(2,1)S(1)} %get-tuple-element.243) | copy-start | bytes 4718596 | tf_op jit(solution)/shard_map/while
  242.7 2.0 copy-start.3
  249.4 2.0 copy-start.5
  251.9 3.3 copy-start.4
  253.6 2.9 copy-start.2
  261.4 6.1 %copy-start.9 = (bf16[2,512,768]{2,1,0:T(8,128)(2,1)}, bf16[2,512,768]{2,1,0:T(8,128)(2,1)S(1)}, u32[]{:S(2)}) copy-start(bf16[2,512,768]{2,1,0:T(8,128)(2,1)S(1)} %get-tuple-element.243) | copy-start | bytes 4718596 | tf_op jit(solution)/shard_map/while
  264.1 2.0 copy-start.3
  270.8 2.0 copy-start.5
  273.3 3.3 copy-start.4
  275.0 2.9 copy-start.2
  282.8 6.1 %copy-start.9 = (bf16[2,512,768]{2,1,0:T(8,128)(2,1)}, bf16[2,512,768]{2,1,0:T(8,128)(2,1)S(1)}, u32[]{:S(2)}) copy-start(bf16[2,512,768]{2,1,0:T(8,128)(2,1)S(1)} %get-tuple-element.243) | copy-start | bytes 4718596 | tf_op jit(solution)/shard_map/while
  285.5 2.0 copy-start.3
  292.2 2.0 copy-start.5
  294.7 3.3 copy-start.4
  296.3 2.9 copy-start.2
  302.2 2.0 copy-start.10
  304.2 6.2 %copy-start.9 = (bf16[2,512,768]{2,1,0:T(8,128)(2,1)}, bf16[2,512,768]{2,1,0:T(8,128)(2,1)S(1)}, u32[]{:S(2)}) copy-start(bf16[2,512,768]{2,1,0:T(8,128)(2,1)S(1)} %get-tuple-element.243) | copy-start | bytes 4718596 | tf_op jit(solution)/shard_map/while
  306.9 2.0 copy-start.3
  313.6 2.0 copy-start.5
  316.1 3.3 copy-start.4
  317.7 2.9 copy-start.2
  325.6 6.1 %copy-start.9 = (bf16[2,512,768]{2,1,0:T(8,128)(2,1)}, bf16[2,512,768]{2,1,0:T(8,128)(2,1)S(1)}, u32[]{:S(2)}) copy-start(bf16[2,512,768]{2,1,0:T(8,128)(2,1)S(1)} %get-tuple-element.243) | copy-start | bytes 4718596 | tf_op jit(solution)/shard_map/while
  328.3 2.0 copy-start.3
  335.0 2.0 copy-start.5
  337.5 3.3 copy-start.4
  339.1 2.9 copy-start.2
  347.0 6.1 %copy-start.9 = (bf16[2,512,768]{2,1,0:T(8,128)(2,1)}, bf16[2,512,768]{2,1,0:T(8,128)(2,1)S(1)}, u32[]{:S(2)}) copy-start(bf16[2,512,768]{2,1,0:T(8,128)(2,1)S(1)} %get-tuple-element.243) | copy-start | bytes 4718596 | tf_op jit(solution)/shard_map/while
  349.6 2.0 copy-start.3
  358.9 3.3 copy-start.4
  360.5 2.9 copy-start.2
  368.3 6.2 %copy-start.9 = (bf16[2,512,768]{2,1,0:T(8,128)(2,1)}, bf16[2,512,768]{2,1,0:T(8,128)(2,1)S(1)}, u32[]{:S(2)}) copy-start(bf16[2,512,768]{2,1,0:T(8,128)(2,1)S(1)} %get-tuple-element.243) | copy-start | bytes 4718596 | tf_op jit(solution)/shard_map/while
  371.0 2.0 copy-start.3
  377.7 2.0 copy-start.5
  380.3 3.3 copy-start.4
  381.9 2.9 copy-start.2
  389.7 6.1 %copy-start.9 = (bf16[2,512,768]{2,1,0:T(8,128)(2,1)}, bf16[2,512,768]{2,1,0:T(8,128)(2,1)S(1)}, u32[]{:S(2)}) copy-start(bf16[2,512,768]{2,1,0:T(8,128)(2,1)S(1)} %get-tuple-element.243) | copy-start | bytes 4718596 | tf_op jit(solution)/shard_map/while
  392.4 2.0 copy-start.3
  401.6 3.3 copy-start.4
  403.3 2.9 copy-start.2
  411.1 6.2 %copy-start.9 = (bf16[2,512,768]{2,1,0:T(8,128)(2,1)}, bf16[2,512,768]{2,1,0:T(8,128)(2,1)S(1)}, u32[]{:S(2)}) copy-start(bf16[2,512,768]{2,1,0:T(8,128)(2,1)S(1)} %get-tuple-element.243) | copy-start | bytes 4718596 | tf_op jit(solution)/shard_map/while
  413.8 2.0 copy-start.3
  420.5 2.0 copy-start.5
  423.0 3.3 copy-start.4
  424.7 2.9 copy-start.2
  432.5 6.1 %copy-start.9 = (bf16[2,512,768]{2,1,0:T(8,128)(2,1)}, bf16[2,512,768]{2,1,0:T(8,128)(2,1)S(1)}, u32[]{:S(2)}) copy-start(bf16[2,512,768]{2,1,0:T(8,128)(2,1)S(1)} %get-tuple-element.243) | copy-start | bytes 4718596 | tf_op jit(solution)/shard_map/while
  435.2 2.0 copy-start.3
  444.4 3.3 copy-start.4
  446.1 2.9 copy-start.2
  453.9 6.1 %copy-start.9 = (bf16[2,512,768]{2,1,0:T(8,128)(2,1)}, bf16[2,512,768]{2,1,0:T(8,128)(2,1)S(1)}, u32[]{:S(2)}) copy-start(bf16[2,512,768]{2,1,0:T(8,128)(2,1)S(1)} %get-tuple-element.243) | copy-start | bytes 4718596 | tf_op jit(solution)/shard_map/while
  456.6 2.0 copy-start.3
  463.3 2.0 copy-start.5
  465.8 3.3 copy-start.4
  467.5 2.9 copy-start.2
  475.3 6.1 %copy-start.9 = (bf16[2,512,768]{2,1,0:T(8,128)(2,1)}, bf16[2,512,768]{2,1,0:T(8,128)(2,1)S(1)}, u32[]{:S(2)}) copy-start(bf16[2,512,768]{2,1,0:T(8,128)(2,1)S(1)} %get-tuple-element.243) | copy-start | bytes 4718596 | tf_op jit(solution)/shard_map/while
  478.0 2.0 copy-start.3
  487.2 3.3 copy-start.4
  488.9 2.9 copy-start.2
  (64 other events, 115.0 us)
Sparse Core Ops, SparseCore 0:
  9.0 230.9 all-gather.1
where the time goes:
time: 511 us; the launch traced here: 506 us
  matrix products  225 us (44%)
  waiting for transfers between devices  199 us (39%)
  local copies, waits for them, and re-layouts  27.7 us (5%)
  other arithmetic  20.9 us (4%)
  between operations  13.4 us (3%)
  starting transfers between devices  10.5 us (2%)
  loops' own time  10.4 us (2%)
    all_gather x1, waiting for transfers between devices, local(): lax.all_gather(own_rows, ('inner', 'outer'), axis=1, tiled=True)  144 us
    dot_general x72, matrix products, head_terms(): jnp.dot(weights, level_set[1], preferred_element_type=jnp.float32)  112 us
    dot_general x72, matrix products, head_terms(): jnp.einsum('td,nd->tn', query_part, level_set[0], preferred_element_type=...  110 us
    ppermute x4, waiting for transfers between devices, partner_2(): return lax.ppermute(block, axis, route)  54.7 us
    reduce_sum x48, other arithmetic, head_terms(): row_total = jnp.sum(expo_rows, axis=1, keepdims=True)  15.6 us
    ppermute x4, starting transfers between devices, partner_2(): return lax.ppermute(block, axis, route)  10.5 us
    another operation x1, loops' own time, local(): merged = lax.map(per_head, jnp.arange(HEADS, dtype=jnp.int32))  10.4 us
  transfers between devices with their start and end apart: 5, of which 5 were waited for; matrix products, arithmetic and copies ran while one was open for 4% of the time, Pallas kernels for 0%

commit v1 on v0

v1 whole, which is shorter than its diff:
```python
import jax
import jax.numpy as jnp
import numpy as np
from jax import lax
from jax.experimental import pallas as pl
from jax.experimental.pallas import tpu as pltpu
from jax.sharding import PartitionSpec as P

HEADS = 12
HEAD_DIM = 64
D = 768
T = 512
MESH = pl.DeviceIdType.MESH
BLK = 256
GROW = 1536

A0, B30, C0, D0, D1 = 512, 576, 640, 704, 736
B20, C1, A1, D2, D3 = 768, 832, 896, 960, 992
A2, B31, C2, D4, D5 = 1024, 1088, 1152, 1216, 1248
A3, B21, C3, D6, D7 = 1280, 1344, 1408, 1472, 1504


def key_weights():
    w = np.ones((10, BLK), np.float32)
    flat = w.reshape(-1)
    tok = np.arange(T)
    for level in range(1, 5):
        flat[:T] += tok % (1 << level) == 0
    for base, top in ((A0, 4), (B30, 3), (B20, 3), (C0, 2), (C1, 2), (C2, 2), (C3, 2)):
        flat[base : base + 32] = top
        flat[base + 32 : base + 64] = top - 1
    flat[A1 : A1 + 64] = 2
    return w


class Links:
    def __init__(self, send_sem, recv_sem):
        self.send_sem, self.recv_sem, self.count, self.sent = send_sem, recv_sem, 0, []

    def make(self, src, dst, device):
        i = self.count
        self.count += 1
        return pltpu.make_async_remote_copy(
            src_ref=src,
            dst_ref=dst,
            send_sem=self.send_sem.at[i],
            recv_sem=self.recv_sem.at[i],
            device_id=device,
            device_id_type=MESH,
        )


def kernel(
    q_hbm, k_hbm, v_hbm, wout_hbm, wt_ref, o_ref,
    ch, snd, qv, qm, acc, ms, blk, rb, wout, att, send_sem, recv_sem, loc_sem,
):
    inner, outer = lax.axis_index("inner"), lax.axis_index("outer")
    y, xh = lax.rem(inner, 4), lax.div(inner, 4)
    core = lax.rem(outer, 2)
    z = lax.rem(lax.div(outer, 2), 4)
    xl = lax.div(outer, 8)
    x = xh * 2 + xl

    def dev(x, y, z, core):
        return (lax.div(x, 2) * 4 + y, lax.rem(x, 2) * 8 + z * 2 + core)

    xs = [lax.rem(x + i, 4) for i in range(4)]
    ys = [y, lax.rem(y, 2) * -2 + 1 + y, lax.rem(y + 2, 4), 3 - y]
    zs = [lax.rem(z + i, 4) for i in range(4)]
    to_core = dev(x, y, z, 1 - core)
    to_x = [None] + [dev(xs[i], y, z, core) for i in (1, 2, 3)]
    to_y = [None] + [dev(x, ys[i], z, core) for i in (1, 2, 3)]
    to_up, to_down = dev(x, y, zs[1], core), dev(x, y, zs[3], core)
    partners = [to_core] + to_x[1:] + to_y[1:] + [to_up, to_down]

    loads = [
        pltpu.make_async_copy(k_hbm, ch.at[0, pl.ds(0, T)], loc_sem.at[0]),
        pltpu.make_async_copy(v_hbm, ch.at[1, pl.ds(0, T)], loc_sem.at[1]),
        pltpu.make_async_copy(q_hbm, qv, loc_sem.at[2]),
        pltpu.make_async_copy(wout_hbm, wout, loc_sem.at[3]),
    ]
    for load in loads:
        load.start()
    barrier = pltpu.get_barrier_semaphore()
    for device in partners:
        pl.semaphore_signal(barrier, inc=1, device_id=device, device_id_type=MESH)

    row = lax.broadcasted_iota(jnp.int32, (BLK, T), 0)
    col = lax.broadcasted_iota(jnp.int32, (BLK, T), 1)
    token = jnp.where(
        row < 32,
        row * 16,
        jnp.where(row < 64, row * 16 - 504, jnp.where(row < 128, row * 8 - 508, row * 4 - 510)),
    )
    pick = jnp.where(col == token, 1.0, 0.0).astype(jnp.bfloat16)
    grow = lax.broadcasted_iota(jnp.int32, (16, T), 0)
    gcol = lax.broadcasted_iota(jnp.int32, (16, T), 1)
    gpick = jnp.where(gcol == (grow - core * 8) * 64, 1.0, 0.0)
    gpick = jnp.where((grow < 8) == (core == 0), gpick, 0.0).astype(jnp.bfloat16)
    for i in range(2):
        loads[i].wait()
        own = ch[i, 0:T, :]
        snd[i] = jnp.dot(pick, own, preferred_element_type=jnp.float32).astype(jnp.bfloat16)
        blk[i] = jnp.dot(gpick, own, preferred_element_type=jnp.float32).astype(jnp.bfloat16)

    links = Links(send_sem, recv_sem)

    def piece(src_row, dst_row, rows, device, from_snd=False):
        src = (snd if from_snd else ch).at[:, pl.ds(src_row, rows)]
        return links.make(src, ch.at[:, pl.ds(dst_row, rows)], device)

    def gpiece(start, rows, device, land=None, part=None):
        part = core if part is None else part
        where = pl.ds(pl.multiple_of(start, 16), rows)
        return links.make(ch.at[part, where], ch.at[part, where], device)

    plane = [GROW + zz * BLK for zz in zs]
    slot = plane[0] + y * 64 + x * 16
    c_a0 = piece(0, A0, 64, to_y[1], True)
    c_b30 = piece(0, B30, 64, to_y[3], True)
    c_c0 = piece(0, C0, 64, to_x[2], True)
    c_d0 = piece(0, D0, 32, to_core, True)
    c_a1 = piece(64, A1, 64, to_y[1], True)
    c_b31 = piece(64, B31, 64, to_y[3], True)
    c_a2 = piece(128, A2, 64, to_y[1], True)
    c_a3 = piece(192, A3, 64, to_y[1], True)
    c_b20 = piece(A0, B20, 64, to_y[3])
    c_c1 = piece(A0, C1, 64, to_x[2])
    c_c2 = piece(B30, C2, 64, to_x[2])
    c_c3 = piece(B20, C3, 64, to_x[2])
    c_b21 = piece(A1, B21, 64, to_y[3])
    c_d1 = piece(A0, D1, 32, to_core)
    c_d2 = piece(B30, D2, 32, to_core)
    c_d3 = piece(B20, D3, 32, to_core)
    c_d4 = piece(C0, D4, 32, to_core)
    c_d5 = piece(C1, D5, 32, to_core)
    c_d6 = piece(C2, D6, 32, to_core)
    c_d7 = piece(C3, D7, 32, to_core)
    e0 = links.make(blk.at[1 - core], rb, to_core)
    e1 = [gpiece(slot, 16, to_x[i]) for i in (1, 2, 3)]
    e2 = [gpiece(plane[0] + y * 64, 64, to_y[i]) for i in (1, 2, 3)]
    e3 = [gpiece(plane[0], BLK, to_up), gpiece(plane[0], BLK, to_down)]
    e4 = [gpiece(plane[3], 128, to_up), gpiece(plane[1] + 128, 128, to_down)]
    f0 = gpiece(plane[0], BLK, to_core)
    f1 = gpiece(plane[1], BLK, to_core)
    f3 = gpiece(plane[3], BLK, to_core)
    f2 = gpiece(plane[2], BLK, to_core)
    everything = [
        c_a0, c_b30, c_c0, c_d0, c_a1, c_b31, c_a2, c_a3, c_b20, c_c1, c_c2, c_c3, c_b21,
        c_d1, c_d2, c_d3, c_d4, c_d5, c_d6, c_d7, e0, *e1, *e2, *e3, *e4, f0, f1, f3, f2,
    ]

    def start(*copies):
        for copy in copies:
            copy.start()

    def arrived(*copies):
        for copy in copies:
            copy.wait_recv()

    pl.semaphore_wait(barrier, len(partners))
    start(e0, c_a0, c_b30, c_d0)

    lane = lax.broadcasted_iota(jnp.int32, (1, 128), 1)
    loads[2].wait()
    for p in range(HEADS // 2):
        q = qv[:, p * 128 : (p + 1) * 128] * jnp.bfloat16(HEAD_DIM**-0.5)
        zero = jnp.zeros_like(q)
        qm[2 * p] = jnp.where(lane < 64, q, zero)
        qm[2 * p + 1] = jnp.where(lane < 64, zero, q)
    acc[...] = jnp.zeros_like(acc)
    ms[...] = jnp.full_like(ms, -1e30)
    arrived(e0)
    ch[core, pl.ds(pl.multiple_of(slot, 16), 16), :] = blk[core] + rb[...]
    start(*e1, c_c0)

    def attend(r0):
        rows = pl.ds(pl.multiple_of(r0, BLK), BLK)
        weight = wt_ref[pl.ds(lax.div(r0, BLK), 1), :]
        for p in range(HEADS // 2):
            keys = ch[0, rows, p * 128 : (p + 1) * 128]
            vals = ch[1, rows, p * 128 : (p + 1) * 128]
            one = jnp.ones_like(vals)
            for h in range(2):
                n = 2 * p + h
                vx = jnp.where(lane < 64, vals, one) if h == 0 else jnp.where(lane < 64, one, vals)
                s = lax.dot_general(
                    qm[n], keys, (((1,), (1,)), ((), ())), preferred_element_type=jnp.float32
                )
                old = ms[n]
                new = jnp.maximum(old, jnp.max(s, axis=1, keepdims=True))
                e = jnp.exp(s - jnp.concatenate([new, new], axis=1)) * weight
                acc[n] = acc[n] * jnp.exp(old - new) + jnp.dot(
                    e.astype(jnp.bfloat16), vx, preferred_element_type=jnp.float32
                )
                ms[n] = new

    order = [0, BLK, A0, plane[0], B20, A2, plane[1], plane[3], A3, plane[2]]

    def step(j, carry):
        @pl.when(j == 1)
        def _():
            arrived(*e1)
            start(*e2, c_a1)

        @pl.when(j == 2)
        def _():
            arrived(c_a0)
            start(c_b20, c_c1, c_d1)
            arrived(c_b30)
            start(c_c2, c_d2, c_b31, c_a2, c_a3)
            arrived(c_c0)
            start(c_d4)
            arrived(c_d0, c_d1)

        @pl.when(j == 3)
        def _():
            arrived(*e2)
            start(*e3, f0)
            arrived(f0)

        @pl.when(j == 4)
        def _():
            arrived(c_b20)
            start(c_c3, c_d3)
            arrived(c_a1)
            start(c_b21)
            arrived(c_c1)
            start(c_d5)
            arrived(c_d2, c_d3)

        @pl.when(j == 5)
        def _():
            arrived(c_a2, c_b31, c_c2)
            start(c_d6)
            arrived(c_d4, c_d5)

        @pl.when(j == 6)
        def _():
            arrived(*e3)
            start(*e4, f1, f3)
            arrived(f1)

        @pl.when(j == 7)
        def _():
            arrived(f3)

        @pl.when(j == 8)
        def _():
            arrived(c_a3, c_b21, c_c3)
            start(c_d7)
            arrived(*e4)
            start(f2)
            arrived(c_d6, c_d7)

        @pl.when(j == 9)
        def _():
            arrived(f2)

        r0 = sum(jnp.where(j == i, at, 0) for i, at in enumerate(order))
        attend(r0)
        return carry

    lax.fori_loop(0, len(order), step, 0)

    for p in range(HEADS // 2):
        lo, hi = acc[2 * p], acc[2 * p + 1]
        both = jnp.where(lane < 64, lo / pltpu.roll(lo, 64, 1), hi / pltpu.roll(hi, 64, 1))
        att[:, p * 128 : (p + 1) * 128] = both.astype(jnp.bfloat16)
    loads[3].wait()
    o_ref[...] = jnp.dot(att[...], wout[...], preferred_element_type=jnp.float32).astype(jnp.bfloat16)
    for copy in everything:
        copy.wait_send()


N_COPIES = 35


def local(queries, key_rows, values, out_weight):
    anywhere = pl.BlockSpec(memory_space=pl.ANY)
    vmem = pl.BlockSpec(memory_space=pltpu.VMEM)
    bf16, f32 = jnp.bfloat16, jnp.float32
    out = pl.pallas_call(
        kernel,
        out_shape=jax.ShapeDtypeStruct((T, D), bf16),
        in_specs=[anywhere] * 4 + [vmem],
        out_specs=vmem,
        scratch_shapes=[
            pltpu.VMEM((2, 2560, D), bf16),
            pltpu.VMEM((2, BLK, D), bf16),
            pltpu.VMEM((T, D), bf16),
            pltpu.VMEM((HEADS, T, 128), bf16),
            pltpu.VMEM((HEADS, T, 128), f32),
            pltpu.VMEM((HEADS, T, 128), f32),
            pltpu.VMEM((2, 16, D), bf16),
            pltpu.VMEM((16, D), bf16),
            pltpu.VMEM((D, D), bf16),
            pltpu.VMEM((T, D), bf16),
            pltpu.SemaphoreType.DMA((N_COPIES,)),
            pltpu.SemaphoreType.DMA((N_COPIES,)),
            pltpu.SemaphoreType.DMA((4,)),
        ],
        compiler_params=pltpu.CompilerParams(
            collective_id=0, has_side_effects=True, vmem_limit_bytes=60 << 20
        ),
    )(queries[0], key_rows[0], values[0], out_weight, jnp.asarray(key_weights()))
    return out[None]


def solution(mesh):
    placed = P("outer", "inner", None)
    return jax.shard_map(
        local, mesh=mesh, in_specs=(placed, placed, placed, P()), out_specs=placed, check_vma=False
    )
```

time: 511 us -> 47.3 us (0.09)
  matrix products: 225 us -> 0 us
  waiting for transfers between devices: 199 us -> 0 us
  Pallas kernels: 0 us -> 45.1 us
  local copies, waits for them, and re-layouts: 27.7 us -> 2.06 us
  other arithmetic: 20.9 us -> 0 us
  between operations: 13.4 us -> 0.01 us
  starting transfers between devices: 10.5 us -> 0 us
  loops' own time: 10.4 us -> 0 us
    dot_general x145 -> x0, matrix products: 225 us -> none  [the longest x72 112 us: head_terms(): jnp.dot(weights, level_set[1], preferred_element_type=jnp.float32)]
    all_gather x1 -> x0, waiting for transfers between devices: 144 us -> none  [local(): lax.all_gather(own_rows, ('inner', 'outer'), axis=1, tiled=True)]
    ppermute x4 -> x0, waiting for transfers between devices: 54.7 us -> none  [partner_2(): return lax.ppermute(block, axis, route)]
    pallas_call x0 -> x1, Pallas kernels: none -> 45.1 us  [local(): pl.pallas_call(kernel, out_shape=jax.ShapeDtypeStruct((T, D), bf16), in_s...]
    slice x5 -> x0, local copies, waits for them, and re-layouts: 17.7 us -> none  [the longest x3 10 us: local(): kv_half = current[:, ::2]]
    reduce_sum x48 -> x0, other arithmetic: 15.6 us -> none  [head_terms(): row_total = jnp.sum(expo_rows, axis=1, keepdims=True)]
    ppermute x4 -> x0, starting transfers between devices: 10.5 us -> none  [partner_2(): return lax.ppermute(block, axis, route)]
    another operation x1 -> x0, loops' own time: 10.4 us -> none  [local(): merged = lax.map(per_head, jnp.arange(HEADS, dtype=jnp.int32))]
  transfers between devices with their start and end apart: 5 -> 0, of which waited for: 5 -> 0; matrix products, arithmetic and copies ran while one was open for 4% -> 0% of each run, Pallas kernels for 0% -> 0%
where the time goes in v1:
time: 47.3 us; the launch traced here: 47.1 us
  Pallas kernels  45.1 us (95%)
  local copies, waits for them, and re-layouts  2.06 us (4%)
    pallas_call x1, Pallas kernels, local(): pl.pallas_call(kernel, out_shape=jax.ShapeDtypeStruct((T, D), bf16), in_s...  45.1 us
    unnamed x1, local copies, waits for them, and re-layouts  2.06 us

profile of v1, /device:TPU:1, one launch (start us, length us, event | category | flops | bytes accessed | tf_op | source)
XLA Modules:
  0.0 47.1 jit_solution(5826904659819225115)
XLA Ops:
  0.0 45.1 %shard_map.55 = bf16[512,768]{1,0:T(8,128)(2,1)} custom-call(bf16[512,768]{1,0:T(8,128)(2,1)} %bitcast.5, bf16[512,768]{1,0:T(8,128)(2,1)} %bitcast.6, bf16[512,768]{1,0:T(8,128)(2,1)} %bitcast.7, bf16[768,768]{1,0:T(8,128)(2,1)} %wout_hbm.1, f32[10,256]{1,0:T(8,128)} %constant.2.clone.wt_ref), custom_call_target="tpu_custom_call" | custom-call | tf_op jit(solution)/shard_map/pallas_call | solution.py:283
  45.1 2.1 %copy.7 = bf16[1,512,768]{2,1,0:T(8,128)(2,1)} copy(bf16[1,512,768]{2,1,0:T(8,128)(2,1)} %bitcast.4) | data formatting | bytes 1572864

commit v2 on v1

v2 whole, which is shorter than its diff:
```python
import jax
import jax.numpy as jnp
from jax import lax
from jax.experimental import pallas as pl
from jax.experimental.pallas import tpu as pltpu
from jax.sharding import PartitionSpec as P

HEADS = 12
HEAD_DIM = 64
D = 768
T = 512
MESH = pl.DeviceIdType.MESH
BLK = 256

ROW = {
    "B30": 512,
    "C0": 576,
    "A0": 640,
    "D1": 704,
    "D0": 736,
    "C3": 768,
    "B21": 832,
    "A2": 896,
    "D7": 960,
    "D2": 992,
    "C2": 1024,
    "A1": 1088,
    "B20": 1152,
    "D3": 1216,
    "D6": 1248,
    "A3": 1280,
    "C1": 1344,
    "B31": 1408,
    "D4": 1472,
    "D5": 1504,
}
GA, GBC, GD = 1536, 1792, 2304
FIRST = ("+e0",)
SECOND = ("+D0", "+A0", "+B30")
STEPS = (
    (256, "-e0", "+e12", "+e11", "+e13", "+C0"),
    (0, "-D0"),
    (512, "-e11", "-e13", "-e12", "+up0", "+e21", "+dn0", "+e23", "+e22", "+A1", "+A3", "+A2", "-A0", "+D1", "+B20", "+B31", "-B30", "+D2", "+C2", "+C1", "-D1", "-D2", "-C0", "+D4", "-e21", "+up1", "+dn1", "-up0", "-dn0", "-e23", "+up3", "+dn3", "-D4"),
    (1536, "-e22", "+fa", "+up2", "+far0", "+dn2", "-fa", "-up1", "-dn1", "+fb", "+far1"),
    (1792, "-C2", "+D6", "-fb", "-A1", "+B21", "-up3", "-dn3", "+far3", "-B20", "+D3", "+C3"),
    (1024, "-D6", "-D3", "-up2", "+far2", "-dn2", "+fc"),
    (2048, "-C1", "+D5", "-fc", "-A3", "-far0", "-far1", "-B31"),
    (1280, "-D5", "-far3", "-far2", "+fd"),
    (2304, "-C3", "+D7", "-A2", "-fd", "-B21"),
    (768, "-D7"),
)


def key_weights():
    shape = (16, BLK)
    flat = lax.broadcasted_iota(jnp.int32, shape, 0) * BLK + lax.broadcasted_iota(jnp.int32, shape, 1)
    own = jnp.where(flat < T, 1.0, 0.0)
    weight = jnp.ones(shape, jnp.float32)
    for level in range(1, 5):
        weight += jnp.where(lax.rem(flat, 1 << level) == 0, own, 0.0)
    for name, top in (("A0", 4), ("B30", 3), ("B20", 3), ("C0", 2), ("C1", 2), ("C2", 2), ("C3", 2), ("A1", 2)):
        base = ROW[name]
        low = top if name == "A1" else top - 1
        weight += jnp.where((flat >= base) & (flat < base + 32), top - 1.0, 0.0)
        weight += jnp.where((flat >= base + 32) & (flat < base + 64), low - 1.0, 0.0)
    return weight


class Links:
    def __init__(self, send_sem, recv_sem):
        self.send_sem, self.recv_sem, self.count, self.sent = send_sem, recv_sem, 0, []

    def make(self, src, dst, device):
        i = self.count
        assert i < N_COPIES
        self.count += 1
        return pltpu.make_async_remote_copy(
            src_ref=src,
            dst_ref=dst,
            send_sem=self.send_sem.at[i],
            recv_sem=self.recv_sem.at[i],
            device_id=device,
            device_id_type=MESH,
        )


def kernel(
    q_hbm, k_hbm, v_hbm, o_ref,
    ch, snd, qv, qm, acc, ms, blk, rb, weights, send_sem, recv_sem, loc_sem,
):
    inner, outer = lax.axis_index("inner"), lax.axis_index("outer")
    y, xh = lax.rem(inner, 4), lax.div(inner, 4)
    core = lax.rem(outer, 2)
    z = lax.rem(lax.div(outer, 2), 4)
    xl = lax.div(outer, 8)
    x = xh * 2 + xl

    def dev(x, y, z, core):
        return (lax.div(x, 2) * 4 + y, lax.rem(x, 2) * 8 + z * 2 + core)

    xs = [lax.rem(x + i, 4) for i in range(4)]
    ys = [y, lax.rem(y, 2) * -2 + 1 + y, lax.rem(y + 2, 4), 3 - y]
    zs = [lax.rem(z + i, 4) for i in range(4)]
    to_core = dev(x, y, z, 1 - core)
    to_x = [None] + [dev(xs[i], y, z, core) for i in (1, 2, 3)]
    to_y = [None] + [dev(x, ys[i], z, core) for i in (1, 2, 3)]
    to_up, to_down = dev(x, y, zs[1], core), dev(x, y, zs[3], core)
    partners = [to_core] + to_x[1:] + to_y[1:] + [to_up, to_down]

    loads = [
        pltpu.make_async_copy(k_hbm, ch.at[0, pl.ds(0, T)], loc_sem.at[0]),
        pltpu.make_async_copy(v_hbm, ch.at[1, pl.ds(0, T)], loc_sem.at[1]),
        pltpu.make_async_copy(q_hbm, qv, loc_sem.at[2]),
    ]
    for load in loads:
        load.start()
    barrier = pltpu.get_barrier_semaphore()
    for device in partners:
        pl.semaphore_signal(barrier, inc=1, device_id=device, device_id_type=MESH)

    grow = lax.broadcasted_iota(jnp.int32, (16, T), 0)
    gcol = lax.broadcasted_iota(jnp.int32, (16, T), 1)
    gpick = jnp.where(gcol == (grow - core * 8) * 64, 1.0, 0.0)
    gpick = jnp.where((grow < 8) == (core == 0), gpick, 0.0).astype(jnp.bfloat16)
    row = lax.broadcasted_iota(jnp.int32, (BLK, T), 0)
    col = lax.broadcasted_iota(jnp.int32, (BLK, T), 1)
    token = jnp.where(
        row < 32,
        row * 16,
        jnp.where(row < 64, row * 16 - 504, jnp.where(row < 128, row * 8 - 508, row * 4 - 510)),
    )
    pick = jnp.where(col == token, 1.0, 0.0).astype(jnp.bfloat16)

    links = Links(send_sem, recv_sem)

    def piece(src_row, dst_row, rows, device, from_snd=False):
        src = snd.at[:, pl.ds(src_row, rows)] if from_snd else ch.at[:, pl.ds(ROW[src_row], rows)]
        return links.make(src, ch.at[:, pl.ds(ROW[dst_row], rows)], device)

    def gpiece(src_row, dst_row, rows, device):
        return links.make(ch.at[core, pl.ds(src_row, rows)], ch.at[core, pl.ds(dst_row, rows)], device)

    copies = {
        "A0": piece(0, "A0", 64, to_y[1], True),
        "B30": piece(0, "B30", 64, to_y[3], True),
        "C0": piece(0, "C0", 64, to_x[2], True),
        "D0": piece(0, "D0", 32, to_core, True),
        "A1": piece(64, "A1", 64, to_y[1], True),
        "B31": piece(64, "B31", 64, to_y[3], True),
        "A2": piece(128, "A2", 64, to_y[1], True),
        "A3": piece(192, "A3", 64, to_y[1], True),
        "B20": piece("A0", "B20", 64, to_y[3]),
        "B21": piece("A1", "B21", 64, to_y[3]),
        "C1": piece("A0", "C1", 64, to_x[2]),
        "C2": piece("B30", "C2", 64, to_x[2]),
        "C3": piece("B20", "C3", 64, to_x[2]),
    }
    for i, name in enumerate(("A0", "B30", "B20", "C0", "C1", "C2", "C3")):
        copies["D%d" % (i + 1)] = piece(name, "D%d" % (i + 1), 32, to_core)
    slot = pl.multiple_of(x * 16, 16)
    copies["e0"] = links.make(blk.at[1 - core], rb, to_core)
    for i in (1, 2, 3):
        copies["e1%d" % i] = gpiece(GA + slot, GA + slot, 16, to_x[i])
        copies["e2%d" % i] = gpiece(GA, GA + i * 64, 64, to_y[i])
    for i in range(4):
        above, below = GBC + i * 128 + 64, GBC + i * 128
        copies["up%d" % i] = gpiece(GA + i * 64, above, 64, to_up)
        copies["dn%d" % i] = gpiece(GA + i * 64, below, 64, to_down)
        copies["far%d" % i] = gpiece(
            below if i % 2 else above, GD + i * 64, 64, to_down if i % 2 else to_up
        )
    for name, at in (("fa", GA), ("fb", GBC), ("fc", GBC + BLK), ("fd", GD)):
        copies[name] = gpiece(at, at, BLK, to_core)

    def act(tokens):
        for token in tokens:
            copy = copies[token[1:]]
            if token[0] == "+":
                copy.start()
            else:
                copy.wait_recv()
                if token == "-e0":
                    ch[core, pl.ds(pl.multiple_of(GA + slot, 16), 16), :] = blk[core] + rb[...]

    for i in range(2):
        loads[i].wait()
        blk[i] = jnp.dot(gpick, ch[i, 0:T, :], preferred_element_type=jnp.float32).astype(jnp.bfloat16)
    pl.semaphore_wait(barrier, len(partners))
    act(FIRST)
    for i in range(2):
        own = ch[i, 0:T, :]
        snd[i] = jnp.dot(pick, own, preferred_element_type=jnp.float32).astype(jnp.bfloat16)
    act(SECOND)

    lane = lax.broadcasted_iota(jnp.int32, (1, 128), 1)
    loads[2].wait()
    for p in range(HEADS // 2):
        q = qv[:, p * 128 : (p + 1) * 128] * jnp.bfloat16(HEAD_DIM**-0.5)
        zero = jnp.zeros_like(q)
        qm[2 * p] = jnp.where(lane < 64, q, zero)
        qm[2 * p + 1] = jnp.where(lane < 64, zero, q)
    weights[...] = key_weights()
    acc[...] = jnp.zeros_like(acc)
    ms[...] = jnp.full_like(ms, -1e30)

    def attend(r0):
        rows = pl.ds(pl.multiple_of(r0, BLK), BLK)
        weight = weights[pl.ds(lax.div(r0, BLK), 1), :]
        for p in range(HEADS // 2):
            keys = ch[0, rows, p * 128 : (p + 1) * 128]
            vals = ch[1, rows, p * 128 : (p + 1) * 128]
            one = jnp.ones_like(vals)
            for h in range(2):
                n = 2 * p + h
                vx = jnp.where(lane < 64, vals, one) if h == 0 else jnp.where(lane < 64, one, vals)
                s = lax.dot_general(
                    qm[n], keys, (((1,), (1,)), ((), ())), preferred_element_type=jnp.float32
                )
                old = ms[n]
                new = jnp.maximum(old, jnp.max(s, axis=1, keepdims=True))
                e = jnp.exp(s - jnp.concatenate([new, new], axis=1)) * weight
                acc[n] = acc[n] * jnp.exp(old - new) + jnp.dot(
                    e.astype(jnp.bfloat16), vx, preferred_element_type=jnp.float32
                )
                ms[n] = new

    def step(j, carry):
        for i, (_, *tokens) in enumerate(STEPS):
            if tokens:
                pl.when(j == i)(lambda tokens=tokens: act(tokens))
        attend(sum(jnp.where(j == i, at, 0) for i, (at, *_) in enumerate(STEPS)))
        return carry

    lax.fori_loop(0, len(STEPS), step, 0)

    for p in range(HEADS // 2):
        lo, hi = acc[2 * p], acc[2 * p + 1]
        both = jnp.where(lane < 64, lo, hi) / pltpu.roll(jnp.where(lane < 64, hi, lo), 64, 1)
        o_ref[:, p * 128 : (p + 1) * 128] = both.astype(jnp.bfloat16)
    for copy in copies.values():
        copy.wait_send()


N_COPIES = 43


def local(queries, key_rows, values, out_weight):
    hbm = pl.BlockSpec(memory_space=pltpu.HBM)
    vmem = pl.BlockSpec(memory_space=pltpu.VMEM)
    bf16, f32 = jnp.bfloat16, jnp.float32
    attended = pl.pallas_call(
        kernel,
        out_shape=jax.ShapeDtypeStruct((T, D), bf16),
        in_specs=[hbm] * 3,
        out_specs=vmem,
        scratch_shapes=[
            pltpu.VMEM((2, 2560, D), bf16),
            pltpu.VMEM((2, BLK, D), bf16),
            pltpu.VMEM((T, D), bf16),
            pltpu.VMEM((HEADS, T, 128), bf16),
            pltpu.VMEM((HEADS, T, 128), f32),
            pltpu.VMEM((HEADS, T, 128), f32),
            pltpu.VMEM((2, 16, D), bf16),
            pltpu.VMEM((16, D), bf16),
            pltpu.VMEM((16, BLK), f32),
            pltpu.SemaphoreType.DMA((N_COPIES,)),
            pltpu.SemaphoreType.DMA((N_COPIES,)),
            pltpu.SemaphoreType.DMA((3,)),
        ],
        compiler_params=pltpu.CompilerParams(
            collective_id=0, has_side_effects=True, vmem_limit_bytes=60 << 20
        ),
    )(queries[0], key_rows[0], values[0])
    return jnp.dot(attended, out_weight, preferred_element_type=f32).astype(bf16)[None]


def solution(mesh):
    placed = P("outer", "inner", None)
    return jax.shard_map(
        local, mesh=mesh, in_specs=(placed, placed, placed, P()), out_specs=placed, check_vma=False
    )
```

time: 47.3 us -> 45.3 us (0.958)
  matrix products: 0 us -> 2.79 us
  Pallas kernels: 45.1 us -> 42.4 us
  local copies, waits for them, and re-layouts: 2.06 us -> 0.01 us
    dot_general x0 -> x1, matrix products: none -> 2.79 us  [local(): jnp.dot(attended, out_weight, preferred_element_type=f32).astype(bf16)[None]]
    pallas_call x1, Pallas kernels: 45.1 us -> 42.4 us  [local(): pl.pallas_call(kernel, out_shape=jax.ShapeDtypeStruct((T, D), bf16), in_s...]
    unnamed x1 -> x2, local copies, waits for them, and re-layouts: 2.06 us -> 0.01 us
where the time goes in v2:
time: 45.3 us; the launch traced here: 45.2 us
  Pallas kernels  42.4 us (94%)
  matrix products  2.79 us (6%)
    pallas_call x1, Pallas kernels, local(): pl.pallas_call(kernel, out_shape=jax.ShapeDtypeStruct((T, D), bf16), in_s...  42.4 us
    dot_general x1, matrix products, local(): jnp.dot(attended, out_weight, preferred_element_type=f32).astype(bf16)[None]  2.79 us

profile of v2, /device:TPU:1, one launch (start us, length us, event | category | flops | bytes accessed | tf_op | source)
XLA Modules:
  0.0 45.2 jit_solution(14125300797501882400)
XLA Ops:
  0.0 0.0 copy-start
  0.0 42.4 %shard_map.46 = bf16[512,768]{1,0:T(8,128)(2,1)} custom-call(bf16[512,768]{1,0:T(8,128)(2,1)} %bitcast.7, bf16[512,768]{1,0:T(8,128)(2,1)} %bitcast.8, bf16[512,768]{1,0:T(8,128)(2,1)} %bitcast.9), custom_call_target="tpu_custom_call" | custom-call | tf_op jit(solution)/shard_map/pallas_call | solution.py:251
  42.4 0.0 copy-done
  42.4 2.8 %fusion = bf16[1,512,768]{2,1,0:T(8,128)(2,1)} fusion(bf16[512,768]{1,0:T(8,128)(2,1)} %shard_map.46, bf16[768,768]{1,0:T(8,128)(2,1)S(1)} %copy-done), kind=kOutput, calls=%fused_computation.1 | convolution fusion | flops 604372992 | bytes 2752512 | tf_op jit(solution)/shard_map/dot_general | solution.py:274
Async XLA Ops:
  0.0 42.4 %copy-start = (bf16[768,768]{1,0:T(8,128)(2,1)S(1)}, bf16[768,768]{1,0:T(8,128)(2,1)}, u32[]{:S(2)}) copy-start(bf16[768,768]{1,0:T(8,128)(2,1)} %param.7) | copy-start | bytes 3538948

commit v3 on v2

--- a/solution.py
+++ b/solution.py
@@ -13,57 +13,72 @@
 BLK = 256
 
 ROW = {
-    "B30": 512,
-    "C0": 576,
-    "A0": 640,
-    "D1": 704,
-    "D0": 736,
-    "C3": 768,
-    "B21": 832,
-    "A2": 896,
-    "D7": 960,
-    "D2": 992,
-    "C2": 1024,
-    "A1": 1088,
-    "B20": 1152,
-    "D3": 1216,
-    "D6": 1248,
-    "A3": 1280,
-    "C1": 1344,
-    "B31": 1408,
-    "D4": 1472,
-    "D5": 1504,
+    "A1": 512,
+    "B30": 576,
+    "C2": 640,
+    "D4": 704,
+    "D2": 736,
+    "A2": 768,
+    "C1": 832,
+    "B21": 896,
+    "D1": 960,
+    "D5": 992,
+    "C3": 1024,
+    "B31": 1088,
+    "A3": 1152,
+    "D7": 1216,
+    "D3": 1248,
+    "A0": 1280,
+    "C0": 1344,
+    "B20": 1408,
+    "D0": 1472,
+    "D6": 1504,
+    "dn0": 1536,
+    "up0": 1600,
+    "g0": 1664,
+    "e21": 1728,
+    "e23": 1792,
+    "dn1": 1856,
+    "far0": 1920,
+    "e22": 1984,
+    "up3": 2048,
+    "up1": 2112,
+    "dn3": 2176,
+    "up2": 2240,
+    "far2": 2304,
+    "far3": 2368,
+    "dn2": 2432,
+    "far1": 2496,
 }
-GA, GBC, GD = 1536, 1792, 2304
-FIRST = ("+e0",)
-SECOND = ("+D0", "+A0", "+B30")
+GLOBAL = 1536
+FIRST = ("+D0", "+e0", "+A0", "+B30",)
 STEPS = (
-    (256, "-e0", "+e12", "+e11", "+e13", "+C0"),
-    (0, "-D0"),
-    (512, "-e11", "-e13", "-e12", "+up0", "+e21", "+dn0", "+e23", "+e22", "+A1", "+A3", "+A2", "-A0", "+D1", "+B20", "+B31", "-B30", "+D2", "+C2", "+C1", "-D1", "-D2", "-C0", "+D4", "-e21", "+up1", "+dn1", "-up0", "-dn0", "-e23", "+up3", "+dn3", "-D4"),
-    (1536, "-e22", "+fa", "+up2", "+far0", "+dn2", "-fa", "-up1", "-dn1", "+fb", "+far1"),
-    (1792, "-C2", "+D6", "-fb", "-A1", "+B21", "-up3", "-dn3", "+far3", "-B20", "+D3", "+C3"),
-    (1024, "-D6", "-D3", "-up2", "+far2", "-dn2", "+fc"),
-    (2048, "-C1", "+D5", "-fc", "-A3", "-far0", "-far1", "-B31"),
-    (1280, "-D5", "-far3", "-far2", "+fd"),
-    (2304, "-C3", "+D7", "-A2", "-fd", "-B21"),
-    (768, "-D7"),
+    (0, "-e0", "+e12", "+e11", "+e13", "+C0", "-D0",),
+    (256, ),
+    (1536, "-e13", "-e11", "-e12", "+e21", "+A1", "+e23", "+e22", "+dn0", "+up0", "+A2", "+A3", "-A0", "+D1", "+B20", "-B30", "+D2", "+C2", "+C1", "-D1", "-D2", "-C0", "+D4", "-e21", "+dn1", "+up1", "-dn0", "-up0", "+f0", "+far0", "-D4", "-e23", "+dn3", "+up3", "-f0",),
+    (512, "-A1", "+B21", "+B31", "-C2", "+D6",),
+    (1280, "-dn1", "+far1", "-up1", "-D6", "-B20", "+D3", "+C3", "-dn3", "-far0", "-e22", "+f1", "+dn2", "+far3", "+up2",),
+    (1792, "-D3", "-C1", "+D5", "-f1", "-up3",),
+    (768, "-A2", "-D5", "-B21", "-far1", "-up2", "+f2", "+far2",),
+    (2048, "-f2", "-dn2", "-C3", "+D7", "-A3",),
+    (1024, "-D7", "-B31", "-far3", "-far2", "+f3",),
+    (2304, "-f3",),
 )
 
 
-def key_weights():
-    shape = (16, BLK)
-    flat = lax.broadcasted_iota(jnp.int32, shape, 0) * BLK + lax.broadcasted_iota(jnp.int32, shape, 1)
-    own = jnp.where(flat < T, 1.0, 0.0)
-    weight = jnp.ones(shape, jnp.float32)
+def key_weights(weights):
+    token = lax.broadcasted_iota(jnp.int32, (T, 128), 0)
+    own = jnp.ones((T, 128), jnp.float32)
     for level in range(1, 5):
-        weight += jnp.where(lax.rem(flat, 1 << level) == 0, own, 0.0)
+        own += jnp.where(lax.rem(token, 1 << level) == 0, 1.0, 0.0)
+    weights[0:T] = own.astype(jnp.bfloat16)
+    weights[T:] = jnp.ones((weights.shape[0] - T, 128), jnp.bfloat16)
+    half = jnp.ones((32, 128), jnp.bfloat16)
     for name, top in (("A0", 4), ("B30", 3), ("B20", 3), ("C0", 2), ("C1", 2), ("C2", 2), ("C3", 2), ("A1", 2)):
         base = ROW[name]
         low = top if name == "A1" else top - 1
-        weight += jnp.where((flat >= base) & (flat < base + 32), top - 1.0, 0.0)
-        weight += jnp.where((flat >= base + 32) & (flat < base + 64), low - 1.0, 0.0)
-    return weight
+        weights[base : base + 32] = half * top
+        weights[base + 32 : base + 64] = half * low
 
 
 class Links:
@@ -157,20 +172,22 @@
     }
     for i, name in enumerate(("A0", "B30", "B20", "C0", "C1", "C2", "C3")):
         copies["D%d" % (i + 1)] = piece(name, "D%d" % (i + 1), 32, to_core)
-    slot = pl.multiple_of(x * 16, 16)
+    own_slot = pl.multiple_of(ROW["g0"] + x * 16, 16)
     copies["e0"] = links.make(blk.at[1 - core], rb, to_core)
     for i in (1, 2, 3):
-        copies["e1%d" % i] = gpiece(GA + slot, GA + slot, 16, to_x[i])
-        copies["e2%d" % i] = gpiece(GA, GA + i * 64, 64, to_y[i])
+        copies["e1%d" % i] = gpiece(own_slot, own_slot, 16, to_x[i])
+        copies["e2%d" % i] = gpiece(ROW["g0"], ROW["e2%d" % i], 64, to_y[i])
     for i in range(4):
-        above, below = GBC + i * 128 + 64, GBC + i * 128
-        copies["up%d" % i] = gpiece(GA + i * 64, above, 64, to_up)
-        copies["dn%d" % i] = gpiece(GA + i * 64, below, 64, to_down)
+        src = ROW["e2%d" % i] if i else ROW["g0"]
+        above, below = ROW["up%d" % i], ROW["dn%d" % i]
+        copies["up%d" % i] = gpiece(src, above, 64, to_up)
+        copies["dn%d" % i] = gpiece(src, below, 64, to_down)
         copies["far%d" % i] = gpiece(
-            below if i % 2 else above, GD + i * 64, 64, to_down if i % 2 else to_up
+            below if i % 2 else above, ROW["far%d" % i], 64, to_down if i % 2 else to_up
         )
-    for name, at in (("fa", GA), ("fb", GBC), ("fc", GBC + BLK), ("fd", GD)):
-        copies[name] = gpiece(at, at, BLK, to_core)
+    for i in range(4):
+        at = GLOBAL + i * BLK
+        copies["f%d" % i] = gpiece(at, at, BLK, to_core)
 
     def act(tokens):
         for token in tokens:
@@ -180,17 +197,17 @@
             else:
                 copy.wait_recv()
                 if token == "-e0":
-                    ch[core, pl.ds(pl.multiple_of(GA + slot, 16), 16), :] = blk[core] + rb[...]
+                    ch[core, pl.ds(own_slot, 16), :] = blk[core] + rb[...]
 
     for i in range(2):
         loads[i].wait()
         blk[i] = jnp.dot(gpick, ch[i, 0:T, :], preferred_element_type=jnp.float32).astype(jnp.bfloat16)
-    pl.semaphore_wait(barrier, len(partners))
-    act(FIRST)
     for i in range(2):
         own = ch[i, 0:T, :]
         snd[i] = jnp.dot(pick, own, preferred_element_type=jnp.float32).astype(jnp.bfloat16)
-    act(SECOND)
+
+    pl.semaphore_wait(barrier, len(partners))
+    act(FIRST)
 
     lane = lax.broadcasted_iota(jnp.int32, (1, 128), 1)
     loads[2].wait()
@@ -199,17 +216,17 @@
         zero = jnp.zeros_like(q)
         qm[2 * p] = jnp.where(lane < 64, q, zero)
         qm[2 * p + 1] = jnp.where(lane < 64, zero, q)
-    weights[...] = key_weights()
+    key_weights(weights)
     acc[...] = jnp.zeros_like(acc)
     ms[...] = jnp.full_like(ms, -1e30)
 
     def attend(r0):
         rows = pl.ds(pl.multiple_of(r0, BLK), BLK)
-        weight = weights[pl.ds(lax.div(r0, BLK), 1), :]
         for p in range(HEADS // 2):
             keys = ch[0, rows, p * 128 : (p + 1) * 128]
             vals = ch[1, rows, p * 128 : (p + 1) * 128]
-            one = jnp.ones_like(vals)
+            one = weights[rows, :]
+            vals = vals * one
             for h in range(2):
                 n = 2 * p + h
                 vx = jnp.where(lane < 64, vals, one) if h == 0 else jnp.where(lane < 64, one, vals)
@@ -218,7 +235,7 @@
                 )
                 old = ms[n]
                 new = jnp.maximum(old, jnp.max(s, axis=1, keepdims=True))
-                e = jnp.exp(s - jnp.concatenate([new, new], axis=1)) * weight
+                e = jnp.exp(s - jnp.concatenate([new, new], axis=1))
                 acc[n] = acc[n] * jnp.exp(old - new) + jnp.dot(
                     e.astype(jnp.bfloat16), vx, preferred_element_type=jnp.float32
                 )
@@ -262,7 +279,7 @@
             pltpu.VMEM((HEADS, T, 128), f32),
             pltpu.VMEM((2, 16, D), bf16),
             pltpu.VMEM((16, D), bf16),
-            pltpu.VMEM((16, BLK), f32),
+            pltpu.VMEM((2560, 128), bf16),
             pltpu.SemaphoreType.DMA((N_COPIES,)),
             pltpu.SemaphoreType.DMA((N_COPIES,)),
             pltpu.SemaphoreType.DMA((3,)),

time: 45.3 us -> 42.9 us (0.947)
  Pallas kernels: 42.4 us -> 39.9 us
    pallas_call x1, Pallas kernels: 42.4 us -> 39.9 us  [local(): pl.pallas_call(kernel, out_shape=jax.ShapeDtypeStruct((T, D), bf16), in_s...]
where the time goes in v3:
time: 42.9 us; the launch traced here: 42.8 us
  Pallas kernels  39.9 us (93%)
  matrix products  2.79 us (7%)
    pallas_call x1, Pallas kernels, local(): pl.pallas_call(kernel, out_shape=jax.ShapeDtypeStruct((T, D), bf16), in_s...  39.9 us
    dot_general x1, matrix products, local(): jnp.dot(attended, out_weight, preferred_element_type=f32).astype(bf16)[None]  2.79 us

profile of v3, /device:TPU:1, one launch (start us, length us, event | category | flops | bytes accessed | tf_op | source)
XLA Modules:
  0.0 42.8 jit_solution(4457726426661985053)
XLA Ops:
  0.0 0.0 copy-start
  0.0 39.9 %shard_map.46 = bf16[512,768]{1,0:T(8,128)(2,1)} custom-call(bf16[512,768]{1,0:T(8,128)(2,1)} %bitcast.7, bf16[512,768]{1,0:T(8,128)(2,1)} %bitcast.8, bf16[512,768]{1,0:T(8,128)(2,1)} %bitcast.9), custom_call_target="tpu_custom_call" | custom-call | tf_op jit(solution)/shard_map/pallas_call | solution.py:268
  40.0 0.0 copy-done
  40.0 2.8 %fusion = bf16[1,512,768]{2,1,0:T(8,128)(2,1)} fusion(bf16[512,768]{1,0:T(8,128)(2,1)} %shard_map.46, bf16[768,768]{1,0:T(8,128)(2,1)S(1)} %copy-done), kind=kOutput, calls=%fused_computation.1 | convolution fusion | flops 604372992 | bytes 2752512 | tf_op jit(solution)/shard_map/dot_general | solution.py:291
Async XLA Ops:
  0.0 40.0 %copy-start = (bf16[768,768]{1,0:T(8,128)(2,1)S(1)}, bf16[768,768]{1,0:T(8,128)(2,1)}, u32[]{:S(2)}) copy-start(bf16[768,768]{1,0:T(8,128)(2,1)} %param.7) | copy-start | bytes 3538948

commit v4 on v3

--- a/solution.py
+++ b/solution.py
@@ -53,15 +53,15 @@
 GLOBAL = 1536
 FIRST = ("+D0", "+e0", "+A0", "+B30",)
 STEPS = (
-    (0, "-e0", "+e12", "+e11", "+e13", "+C0", "-D0",),
-    (256, ),
-    (1536, "-e13", "-e11", "-e12", "+e21", "+A1", "+e23", "+e22", "+dn0", "+up0", "+A2", "+A3", "-A0", "+D1", "+B20", "-B30", "+D2", "+C2", "+C1", "-D1", "-D2", "-C0", "+D4", "-e21", "+dn1", "+up1", "-dn0", "-up0", "+f0", "+far0", "-D4", "-e23", "+dn3", "+up3", "-f0",),
+    (256, "-e0", "+e12", "+e11", "+e13", "+C0", "-D0",),
+    (0, "-e13", "-e11", "-e12", "+e21", "+A1", "+e23", "+e22", "+dn0", "+up0", "+A2",),
+    (1536, "+A3", "-A0", "+D1", "+B20", "-B30", "+D2", "+C2", "+C1", "-D1", "-D2", "-C0", "+D4", "-e21", "+dn1", "+up1", "-dn0", "-up0", "+f0", "+far0", "-D4", "-e23", "+dn3", "+up3", "-f0",),
     (512, "-A1", "+B21", "+B31", "-C2", "+D6",),
     (1280, "-dn1", "+far1", "-up1", "-D6", "-B20", "+D3", "+C3", "-dn3", "-far0", "-e22", "+f1", "+dn2", "+far3", "+up2",),
     (1792, "-D3", "-C1", "+D5", "-f1", "-up3",),
     (768, "-A2", "-D5", "-B21", "-far1", "-up2", "+f2", "+far2",),
-    (2048, "-f2", "-dn2", "-C3", "+D7", "-A3",),
-    (1024, "-D7", "-B31", "-far3", "-far2", "+f3",),
+    (2048, "-f2", "-dn2", "-C3", "+D7",),
+    (1024, "-A3", "-D7", "-B31", "-far3", "-far2", "+f3",),
     (2304, "-f3",),
 )
 
@@ -285,7 +285,7 @@
             pltpu.SemaphoreType.DMA((3,)),
         ],
         compiler_params=pltpu.CompilerParams(
-            collective_id=0, has_side_effects=True, vmem_limit_bytes=60 << 20
+            collective_id=0, has_side_effects=True, vmem_limit_bytes=53 << 20
         ),
     )(queries[0], key_rows[0], values[0])
     return jnp.dot(attended, out_weight, preferred_element_type=f32).astype(bf16)[None]

time: 42.9 us -> 40.7 us (0.949)
  matrix products: 2.79 us -> 1.66 us
  Pallas kernels: 39.9 us -> 39 us
    dot_general x1, matrix products: 2.79 us -> 1.66 us  [local(): jnp.dot(attended, out_weight, preferred_element_type=f32).astype(bf16)[None]]
    pallas_call x1, Pallas kernels: 39.9 us -> 39 us  [local(): pl.pallas_call(kernel, out_shape=jax.ShapeDtypeStruct((T, D), bf16), in_s...]
where the time goes in v4:
time: 40.7 us; the launch traced here: 40.6 us
  Pallas kernels  39 us (96%)
  matrix products  1.66 us (4%)
    pallas_call x1, Pallas kernels, local(): pl.pallas_call(kernel, out_shape=jax.ShapeDtypeStruct((T, D), bf16), in_s...  39 us
    dot_general x1, matrix products, local(): jnp.dot(attended, out_weight, preferred_element_type=f32).astype(bf16)[None]  1.66 us

profile of v4, /device:TPU:1, one launch (start us, length us, event | category | flops | bytes accessed | tf_op | source)
XLA Modules:
  0.0 40.6 jit_solution(1057790791331140399)
XLA Ops:
  0.0 0.0 copy-start
  0.0 39.0 %shard_map.46 = bf16[512,768]{1,0:T(8,128)(2,1)S(1)} custom-call(bf16[512,768]{1,0:T(8,128)(2,1)} %bitcast.7, bf16[512,768]{1,0:T(8,128)(2,1)} %bitcast.8, bf16[512,768]{1,0:T(8,128)(2,1)} %bitcast.9), custom_call_target="tpu_custom_call" | custom-call | tf_op jit(solution)/shard_map/pallas_call | solution.py:268
  39.0 0.0 copy-done
  39.0 1.7 %fusion = bf16[1,512,768]{2,1,0:T(8,128)(2,1)} fusion(bf16[512,768]{1,0:T(8,128)(2,1)S(1)} %shard_map.46, bf16[768,768]{1,0:T(8,128)(2,1)S(1)} %copy-done), kind=kOutput, calls=%fused_computation.1 | convolution fusion | flops 604372992 | bytes 2752512 | tf_op jit(solution)/shard_map/dot_general | solution.py:291
Async XLA Ops:
  0.0 39.0 %copy-start = (bf16[768,768]{1,0:T(8,128)(2,1)S(1)}, bf16[768,768]{1,0:T(8,128)(2,1)}, u32[]{:S(2)}) copy-start(bf16[768,768]{1,0:T(8,128)(2,1)} %param.7) | copy-start | bytes 3538948

commit v5 on v4

--- a/solution.py
+++ b/solution.py
@@ -206,6 +206,9 @@
         own = ch[i, 0:T, :]
         snd[i] = jnp.dot(pick, own, preferred_element_type=jnp.float32).astype(jnp.bfloat16)
 
+    key_weights(weights)
+    acc[...] = jnp.zeros_like(acc)
+    ms[...] = jnp.full_like(ms, -1e30)
     pl.semaphore_wait(barrier, len(partners))
     act(FIRST)
 
@@ -216,9 +219,6 @@
         zero = jnp.zeros_like(q)
         qm[2 * p] = jnp.where(lane < 64, q, zero)
         qm[2 * p + 1] = jnp.where(lane < 64, zero, q)
-    key_weights(weights)
-    acc[...] = jnp.zeros_like(acc)
-    ms[...] = jnp.full_like(ms, -1e30)
 
     def attend(r0):
         rows = pl.ds(pl.multiple_of(r0, BLK), BLK)

time: 40.7 us -> 41.1 us (level)
  no operation moved by 1% of the time
where the time goes in v5:
time: 41.1 us; the launch traced here: 41 us
  Pallas kernels  39.3 us (96%)
  matrix products  1.66 us (4%)
    pallas_call x1, Pallas kernels, local(): pl.pallas_call(kernel, out_shape=jax.ShapeDtypeStruct((T, D), bf16), in_s...  39.3 us
    dot_general x1, matrix products, local(): jnp.dot(attended, out_weight, preferred_element_type=f32).astype(bf16)[None]  1.66 us

profile of v5, /device:TPU:1, one launch (start us, length us, event | category | flops | bytes accessed | tf_op | source)
XLA Modules:
  0.0 41.0 jit_solution(8418282702282302387)
XLA Ops:
  0.0 0.0 copy-start
  0.0 39.3 %shard_map.46 = bf16[512,768]{1,0:T(8,128)(2,1)S(1)} custom-call(bf16[512,768]{1,0:T(8,128)(2,1)} %bitcast.7, bf16[512,768]{1,0:T(8,128)(2,1)} %bitcast.8, bf16[512,768]{1,0:T(8,128)(2,1)} %bitcast.9), custom_call_target="tpu_custom_call" | custom-call | tf_op jit(solution)/shard_map/pallas_call | solution.py:268
  39.3 0.0 copy-done
  39.3 1.7 %fusion = bf16[1,512,768]{2,1,0:T(8,128)(2,1)} fusion(bf16[512,768]{1,0:T(8,128)(2,1)S(1)} %shard_map.46, bf16[768,768]{1,0:T(8,128)(2,1)S(1)} %copy-done), kind=kOutput, calls=%fused_computation.1 | convolution fusion | flops 604372992 | bytes 2752512 | tf_op jit(solution)/shard_map/dot_general | solution.py:291
Async XLA Ops:
  0.0 39.3 %copy-start = (bf16[768,768]{1,0:T(8,128)(2,1)S(1)}, bf16[768,768]{1,0:T(8,128)(2,1)}, u32[]{:S(2)}) copy-start(bf16[768,768]{1,0:T(8,128)(2,1)} %param.7) | copy-start | bytes 3538948
